TPU v7x, 32 devices: a whole 2x2x4 slice. The times are simulated.
32 devices in a mesh: groups: 2 (over x), tm: 8 (over z, y), space: 2 (over core).
Axes of the slice: x: 2, y: 2, z: 4, core: 2. Of those that a mesh axis runs over, the one named last changes fastest.
Arguments:
- latents: bfloat16 [32, 12, 80, 2240], P(('groups', 'tm'), 'space'), parts along dimension 0, may hold values from -8 to 8
- proj_weight: bfloat16 [2240, 3360], P('tm'), may hold values from -0.125 to 0.125
Outputs:
- attended: bfloat16 [32, 12, 80, 1120], P(('groups', 'tm'), 'space'), parts along dimension 0
There are 2 independent parts, one for each index of `groups`. A program takes and returns all parts, laid end to end along the dimension named above; an argument that names none is the same for every part. Nothing has to cross between parts.
All inputs are finite; a program needn't handle non-finite values.
Results may differ from a plain program's by a relative error of at most 0.0034.
Values may be sent and summed in bfloat16 or wider, within the bound.
A program may use at most 128 MiB of HBM per device.

v0:
```python
import jax
import jax.numpy as jnp
from jax import lax
from jax.sharding import PartitionSpec as P

HEADS = 10
HEAD = 112


def entering(value, axis, join, neutral):
    count, mine = (lax.axis_size(axis), lax.axis_index(axis))
    pieces = jax.tree.map(lambda part: lax.all_gather(part, axis), value)
    subtotal = jax.tree.map(
        lambda part, zero: jnp.full_like(part, 0) + jnp.asarray(zero, part.dtype), value, neutral
    )

    def hop(position, subtotal):
        longer = join(subtotal, jax.tree.map(lambda part: part[position], pieces))
        return jax.tree.map(lambda new, old: jnp.where(position < mine, new, old), longer, subtotal)

    return lax.fori_loop(0, count - 1, hop, subtotal)


def add_pairs(earlier, later):
    return (earlier[0] + later[0], earlier[1] + later[1])


def make_adder(flat, shard_rows):
    return jnp.dot(flat, shard_rows, preferred_element_type=jnp.float32)


def project_rows(flat, columns):
    return make_adder(flat, lax.all_gather(columns, "tm", axis=0, tiled=True))


def local_states(projected, heads_here):
    count = projected.shape[0]
    split = projected.astype(jnp.bfloat16).reshape(count, 3, heads_here, HEAD)
    queries = jax.nn.relu(split[:, 0])
    key_feats = jax.nn.relu(split[:, 1])
    values = split[:, 2]
    states = jnp.einsum("nhe,nhf->hef", key_feats, values, preferred_element_type=jnp.float32)
    key_sums = jnp.sum(key_feats, axis=0, dtype=jnp.float32)
    return (queries, states, key_sums)


def apply_states(queries, states, key_sums):
    numerator = jnp.einsum(
        "nhe,hef->nhf", queries, states.astype(jnp.bfloat16), preferred_element_type=jnp.float32
    )
    denominator = jnp.einsum(
        "nhe,he->nh", queries.astype(jnp.float32), key_sums, precision=lax.Precision.HIGHEST
    )
    return (numerator / (denominator[:, :, None] + 1.0)).astype(jnp.bfloat16)


def on_device(latents, proj_weight):
    frame_count, band_rows, column_count, channels = latents.shape
    shard_depth = proj_weight.shape[0]
    band_count = lax.axis_size("space")
    band_index = lax.axis_index("space")
    heads_here = HEADS // band_count
    grouped = proj_weight.reshape(shard_depth, 3, band_count, heads_here * HEAD)
    own_columns = lax.dynamic_index_in_dim(grouped, band_index, 2, keepdims=False)
    own_columns = own_columns.reshape(shard_depth, 3 * heads_here * HEAD)
    both_bands = lax.all_gather(latents, "space", axis=1, tiled=True)
    joined_rows = both_bands.shape[1]
    count = frame_count * joined_rows * column_count
    flat = both_bands.reshape(count, channels)
    projected = project_rows(flat, own_columns)
    queries, states, key_sums = local_states(projected, heads_here)
    identity = (jnp.zeros_like(states), jnp.zeros_like(key_sums))
    earlier = entering((states, key_sums), "tm", add_pairs, identity)
    attended = apply_states(queries, states + earlier[0], key_sums + earlier[1])
    attended = attended.reshape(frame_count, joined_rows, column_count, heads_here * HEAD)
    return lax.all_to_all(attended, "space", split_axis=1, concat_axis=3, tiled=True)


def solution(mesh):
    return jax.shard_map(
        on_device,
        mesh=mesh,
        in_specs=(P(("groups", "tm"), "space", None, None), P("tm", None)),
        out_specs=P(("groups", "tm"), "space", None, None),
        check_vma=False,
    )
```

profile of v0, /device:TPU:0, one launch (start us, length us, event | category | flops | bytes accessed | tf_op | source)
XLA Modules:
  0.0 274.9 jit_solution(16868224540163675632)
XLA Ops:
  6.5 0.7 all-gather.9.cloned.1.call-update
  7.3 0.0 all-gather.7.cloned.1.call-start
  7.3 5.4 %reshape.22 = bf16[280,3,2,560]{3,2,1,0:T(2,128)(2,1)S(1)} reshape(bf16[280,3360]{1,0:T(8,128)(2,1)} %param.5) | data formatting | bytes 3763200 | tf_op jit(solution)/shard_map/reshape | solution.py:63
  12.7 3.6 %constant_dynamic-slice_fusion = bf16[280,3,1,560]{3,2,1,0:T(2,128)(2,1)} fusion(bf16[280,3,2,560]{3,2,1,0:T(2,128)(2,1)S(1)} %reshape.22, s32[]{:T(128)S(6)} %select_n.42), kind=kLoop, calls=%fused_computation.21 | loop fusion | bytes 1881604 | tf_op jit(solution)/shard_map/jit(dynamic_index_in_dim)/dynamic_slice | solution.py:64
  16.3 6.2 %copy.25 = bf16[280,3,1,560]{0,3,1,2:T(8,128)(2,1)S(1)} copy(bf16[280,3,1,560]{3,2,1,0:T(2,128)(2,1)} %constant_dynamic-slice_fusion) | data formatting | bytes 1881600
  22.4 2.3 copy.13
  24.7 0.0 all-gather.7.cloned.1.call-update
  24.7 0.0 all-gather.11.cloned.1.call-start
  24.8 6.2 %all-gather.9.cloned.1.call-done = bf16[2,12,80,2240]{3,2,1,0:T(8,128)(2,1)} async-done(((bf16[2,6,80,2240]{3,2,1,0:T(8,128)(2,1)}), bf16[2,12,80,2240]{3,2,1,0:T(8,128)(2,1)}) %all-gather.9.cloned.1.call-update) | async-done | bytes 8601616 | tf_op jit(solution)/shard_map/all_gather | solution.py:66
  31.0 123.3 %all-gather.7.cloned.1.call-done = bf16[2240,1680]{1,0:T(8,128)(2,1)} async-done(((bf16[280,1680]{1,0:T(8,128)(2,1)}), bf16[2240,1680]{1,0:T(8,128)(2,1)}) %all-gather.7.cloned.1.call-update) | async-done | bytes 7526416 | tf_op jit(solution)/shard_map/all_gather | solution.py:33
  154.3 22.4 %convolution_convert_fusion = bf16[1680,1920]{1,0:T(8,128)(2,1)S(1)} fusion(bf16[2240,1680]{1,0:T(8,128)(2,1)} %all-gather.7.cloned.1.call-done, bf16[1920,2240]{1,0:T(8,128)(2,1)} %bitcast.54), kind=kOutput, calls=%fused_computation.2 | convolution fusion | flops 14453913600 | bytes 22579200 | tf_op jit(solution)/shard_map/dot_general | solution.py:29
  176.8 2.7 copy-done
  179.5 1.5 fusion.2
  181.0 0.0 all-gather.11.cloned.1.call-update
  181.0 2.1 convert_reduce_fusion
  183.1 31.0 %all-gather.2 = f32[8,5,112]{2,1,0:T(8,128)S(1)} all-gather(f32[1,5,112]{2,1,0:T(8,128)S(1)} %bitcast.53), channel_id=3, replica_groups=mesh['groups'=2,'tm'=8,'space'=2] {'tm'}, dimensions={0}, use_global_device_ids=true | all-gather | bytes 20160 | tf_op jit(solution)/shard_map/all_gather | solution.py:12
  214.1 16.5 %all-gather.11.cloned.1.call-done = f32[40,112,112]{2,1,0:T(8,128)} async-done(((f32[5,112,112]{2,1,0:T(8,128)}), f32[40,112,112]{2,1,0:T(8,128)}) %all-gather.11.cloned.1.call-update) | async-done | bytes 2007056 | tf_op jit(solution)/shard_map/all_gather | solution.py:12
  230.6 7.6 %while.16 = (s32[]{:T(128)}, f32[5,112,112]{2,1,0:T(8,128)S(1)}, f32[5,112]{1,0:T(8,128)S(1)}, s32[]{:T(128)}, f32[8,5,112,112]{3,2,1,0:T(8,128)}, /*index=5*/f32[8,5,112]{2,1,0:T(8,128)S(1)}, s32[]{:T(128)}, s32[]{:T(128)}) while((s32[]{:T(128)}, f32[5,112,112]{2,1,0:T(8,128)S(1)}, f32[5,112]{1,0:T(8,128)S(1)}, s32[]{:T(128)}, ...), condition=%wide.region_2.3_spmd.clone, body=%wide.region_1.2_spmd.clone.sunk | while | flops 189844 | bytes 759475 | solution.py:21
  230.6 1.0 add_select_fusion.4
  231.7 1.0 add_select_fusion.4
  232.8 1.0 add_select_fusion.4
  233.9 1.0 add_select_fusion.4
  235.0 1.0 add_select_fusion.4
  236.1 1.0 add_select_fusion.4
  237.1 1.0 add_select_fusion.4
  238.2 2.6 fusion.5
  240.9 2.4 fusion
  243.3 8.0 %reshape.34 = bf16[2,12,80,560]{2,1,0,3:T(8,128)(2,1)} reshape(bf16[1920,5,112]{0,2,1:T(8,128)(2,1)S(1)} %fusion) | data formatting | bytes 4300800 | tf_op jit(solution)/shard_map/reshape | solution.py:75
  251.4 6.0 %copy.16 = bf16[2,12,80,560]{3,2,0,1:T(8,128)(2,1)S(1)} copy(bf16[2,12,80,560]{2,1,0,3:T(8,128)(2,1)} %reshape.34) | data formatting | bytes 4300800 | tf_op jit(solution)/shard_map/reshape | solution.py:75
  257.3 5.7 %all_to_all.18 = bf16[2,12,80,560]{3,2,0,1:T(8,128)(2,1)S(1)} all-to-all(bf16[2,12,80,560]{3,2,0,1:T(8,128)(2,1)S(1)} %copy.16), channel_id=1, replica_groups=mesh['groups'=2,'tm'=8,'space'=2] {'space'}, dimensions={1} | all-to-all | bytes 4300800 | tf_op jit(solution)/shard_map/all_to_all | solution.py:76
  263.0 2.5 copy.18
  265.6 2.9 %all_to_all.16 = bf16[2,6,80,1120]{3,2,1,0:T(8,128)(2,1)} reshape(bf16[2,6,80,2,560]{4,3,2,1,0:T(2,128)(2,1)S(1)} %copy.18) | data formatting | bytes 4300800 | tf_op jit(solution)/shard_map/all_to_all | solution.py:76
  (15 shorter events, 0.1 us)
Async XLA Ops:
  6.5 24.5 %all-gather.9.cloned.1.call-start = ((), (), s32[]{:S(2)}) async-start(), calls=%async_computation.2 | async-start | bytes 13271040 | tf_op jit(solution)/shard_map/all_gather | solution.py:66
  7.3 147.1 %all-gather.7.cloned.1.call-start = ((), (), s32[]{:S(2)}) async-start(), calls=%async_computation.1 | async-start | bytes 9031680 | tf_op jit(solution)/shard_map/all_gather | solution.py:33
  24.7 205.9 %all-gather.11.cloned.1.call-start = ((), (), s32[]{:S(2)}) async-start(), calls=%async_computation.3 | async-start | bytes 2580480 | tf_op jit(solution)/shard_map/all_gather | solution.py:12
  176.8 2.7 copy-start
  238.2 2.7 copy-start.1
Sparse Core Ops, SparseCore 0:
  8.9 22.1 all-gather.8
  33.2 121.0 all-gather.6
  181.1 49.4 all-gather.10
where the time goes:
time: 276 us; the launch traced here: 275 us
  waiting for transfers between devices  147 us (53%)
  local copies, waits for them, and re-layouts  39.5 us (14%)
  blocking collectives  36.7 us (13%)
  matrix products  28.9 us (10%)
  between operations  13.2 us (5%)
  other arithmetic  9.53 us (3%)
    all_gather x1, waiting for transfers between devices, project_rows(): return make_adder(flat, lax.all_gather(columns, 'tm', axis=0, tiled=True))  123 us
    all_gather x1, blocking collectives, entering(): pieces = jax.tree.map(lambda part: lax.all_gather(part, axis), value)  31 us
    dot_general x1, matrix products, make_adder(): return jnp.dot(flat, shard_rows, preferred_element_type=jnp.float32)  22.4 us
    all_gather x1, waiting for transfers between devices, entering(): pieces = jax.tree.map(lambda part: lax.all_gather(part, axis), value)  16.5 us
    reshape x2, local copies, waits for them, and re-layouts, on_device(): attended.reshape(frame_count, joined_rows, column_count, heads_here * HEAD)  14 us
    unnamed x5, local copies, waits for them, and re-layouts  8.87 us
    select_n x14, other arithmetic, hop(): jnp.where(position < mine, new, old)  7.4 us
    all_gather x1, waiting for transfers between devices, on_device(): both_bands = lax.all_gather(latents, 'space', axis=1, tiled=True)  6.23 us
  transfers between devices with their start and end apart: 3, of which 3 were waited for; matrix products, arithmetic and copies ran while one was open for 7% of the time, Pallas kernels for 0%

commit v1 on v0

--- a/solution.py
+++ b/solution.py
@@ -5,6 +5,18 @@
 
 HEADS = 10
 HEAD = 112
+
+
+def gather_around(array, axis, dim):
+    ways, here, step = (lax.axis_size(axis), lax.axis_index(axis), array.shape[dim])
+    dims = [n * ways if d == dim else n for d, n in enumerate(array.shape)]
+    full = lax.dynamic_update_slice_in_dim(
+        jnp.zeros(dims, array.dtype), array, here * step, axis=dim
+    )
+    for far in range(1, ways):
+        array = lax.ppermute(array, axis, [(d, (d + 1) % ways) for d in range(ways)])
+        full = lax.dynamic_update_slice_in_dim(full, array, (here - far) % ways * step, axis=dim)
+    return full
 
 
 def entering(value, axis, join, neutral):
@@ -30,7 +42,7 @@
 
 
 def project_rows(flat, columns):
-    return make_adder(flat, lax.all_gather(columns, "tm", axis=0, tiled=True))
+    return make_adder(flat, gather_around(columns, "tm", 0))
 
 
 def local_states(projected, heads_here):

time: 276 us -> 428 us (1.55)
  local copies, waits for them, and re-layouts: 39.5 us -> 167 us
  waiting for transfers between devices: 147 us -> 167 us
    ppermute x0 -> x7, waiting for transfers between devices: none -> 147 us  [gather_around(): lax.ppermute(array, axis, [(d, (d + 1) % ways) for d in range(ways)])]
    all_gather x1 -> x0, waiting for transfers between devices: 123 us -> none  [project_rows(): return make_adder(flat, lax.all_gather(columns, 'tm', axis=0, tiled=True))]
    dynamic_update_slice x0 -> x8, local copies, waits for them, and re-layouts: none -> 108 us  [the longest x7 95.9 us: gather_around(): lax.dynamic_update_slice_in_dim(full, array, (here - far) % ways * step,...]
    ppermute x0 -> x7, local copies, waits for them, and re-layouts: none -> 13.3 us  [gather_around(): lax.ppermute(array, axis, [(d, (d + 1) % ways) for d in range(ways)])]
    all_gather x1, waiting for transfers between devices: 6.23 us -> 0.01 us  [on_device(): both_bands = lax.all_gather(latents, 'space', axis=1, tiled=True)]
    unnamed x5 -> x17, local copies, waits for them, and re-layouts: 8.87 us -> 11.7 us
  transfers between devices with their start and end apart: 3 -> 9, of which waited for: 3 -> 7; matrix products, arithmetic and copies ran while one was open for 7% -> 34% of each run, Pallas kernels for 0% -> 0%
where the time goes in v1:
time: 428 us; the launch traced here: 424 us
  waiting for transfers between devices  167 us (39%)
  local copies, waits for them, and re-layouts  167 us (39%)
  blocking collectives  36.9 us (9%)
  matrix products  27.3 us (6%)
  between operations  13.6 us (3%)
  other arithmetic  9.53 us (2%)
    ppermute x7, waiting for transfers between devices, gather_around(): lax.ppermute(array, axis, [(d, (d + 1) % ways) for d in range(ways)])  147 us
    dynamic_update_slice x7, local copies, waits for them, and re-layouts, gather_around(): lax.dynamic_update_slice_in_dim(full, array, (here - far) % ways * step,...  95.9 us
    all_gather x1, blocking collectives, entering(): pieces = jax.tree.map(lambda part: lax.all_gather(part, axis), value)  31.2 us
    dot_general x1, matrix products, make_adder(): return jnp.dot(flat, shard_rows, preferred_element_type=jnp.float32)  20.8 us
    all_gather x1, waiting for transfers between devices, entering(): pieces = jax.tree.map(lambda part: lax.all_gather(part, axis), value)  18.3 us
    reshape x2, local copies, waits for them, and re-layouts, on_device(): attended.reshape(frame_count, joined_rows, column_count, heads_here * HEAD)  14 us
    ppermute x7, local copies, waits for them, and re-layouts, gather_around(): lax.ppermute(array, axis, [(d, (d + 1) % ways) for d in range(ways)])  13.3 us
    dynamic_update_slice x1, local copies, waits for them, and re-layouts, gather_around(): lax.dynamic_update_slice_in_dim(jnp.zeros(dims, array.dtype), array, here...  12.4 us
  transfers between devices with their start and end apart: 9, of which 7 were waited for; matrix products, arithmetic and copies ran while one was open for 34% of the time, Pallas kernels for 0%

profile of v1, /device:TPU:0, one launch (start us, length us, event | category | flops | bytes accessed | tf_op | source)
XLA Modules:
  0.0 424.1 jit_solution(4813444243621213190)
XLA Ops:
  7.3 5.4 %reshape.22 = bf16[280,3,2,560]{3,2,1,0:T(2,128)(2,1)S(1)} reshape(bf16[280,3360]{1,0:T(8,128)(2,1)} %param.5) | data formatting | bytes 3763200 | tf_op jit(solution)/shard_map/reshape | solution.py:75
  12.7 3.6 constant_dynamic-slice_fusion
  16.3 6.2 %copy.32 = bf16[280,3,1,560]{0,3,1,2:T(8,128)(2,1)S(1)} copy(bf16[280,3,1,560]{3,2,1,0:T(2,128)(2,1)} %constant_dynamic-slice_fusion) | data formatting | bytes 1881600
  24.0 3.1 collective-permute-start
  27.1 25.2 %collective-permute-done = bf16[280,1680]{1,0:T(8,128)(2,1)S(1)} collective-permute-done((bf16[280,1680]{1,0:T(8,128)(2,1)S(1)}, bf16[280,1680]{1,0:T(8,128)(2,1)S(1)}, u32[]{:S(2)}, u32[]{:S(2)}) %collective-permute-start) | collective-permute-done | bytes 940832 | tf_op jit(solution)/shard_map/ppermute | solution.py:17
  52.4 26.1 %collective-permute-done.1 = bf16[280,1680]{1,0:T(8,128)(2,1)S(1)} collective-permute-done((bf16[280,1680]{1,0:T(8,128)(2,1)S(1)}, bf16[280,1680]{1,0:T(8,128)(2,1)S(1)}, u32[]{:S(2)}, u32[]{:S(2)}) %collective-permute-start.1) | collective-permute-done | bytes 940832 | tf_op jit(solution)/shard_map/ppermute | solution.py:17
  78.5 25.3 %collective-permute-done.2 = bf16[280,1680]{1,0:T(8,128)(2,1)S(1)} collective-permute-done((bf16[280,1680]{1,0:T(8,128)(2,1)S(1)}, bf16[280,1680]{1,0:T(8,128)(2,1)S(1)}, u32[]{:S(2)}, u32[]{:S(2)}) %collective-permute-start.2) | collective-permute-done | bytes 940832 | tf_op jit(solution)/shard_map/ppermute | solution.py:17
  104.8 24.4 %collective-permute-done.3 = bf16[280,1680]{1,0:T(8,128)(2,1)S(1)} collective-permute-done((bf16[280,1680]{1,0:T(8,128)(2,1)S(1)}, bf16[280,1680]{1,0:T(8,128)(2,1)S(1)}, u32[]{:S(2)}, u32[]{:S(2)}) %collective-permute-start.3) | collective-permute-done | bytes 940832 | tf_op jit(solution)/shard_map/ppermute | solution.py:17
  130.2 23.6 %collective-permute-done.4 = bf16[280,1680]{1,0:T(8,128)(2,1)S(1)} collective-permute-done((bf16[280,1680]{1,0:T(8,128)(2,1)S(1)}, bf16[280,1680]{1,0:T(8,128)(2,1)S(1)}, u32[]{:S(2)}, u32[]{:S(2)}) %collective-permute-start.4) | collective-permute-done | bytes 940832 | tf_op jit(solution)/shard_map/ppermute | solution.py:17
  154.7 22.8 %collective-permute-done.5 = bf16[280,1680]{1,0:T(8,128)(2,1)} collective-permute-done((bf16[280,1680]{1,0:T(8,128)(2,1)S(1)}, bf16[280,1680]{1,0:T(8,128)(2,1)}, u32[]{:S(2)}, u32[]{:S(2)}) %collective-permute-start.5) | collective-permute-done | bytes 940832 | tf_op jit(solution)/shard_map/ppermute | solution.py:17
  177.5 3.5 broadcast_in_dim.10
  181.1 12.4 %dynamic_update_slice.24 = bf16[2240,1680]{0,1:T(8,128)(2,1)} dynamic-update-slice(bf16[2240,1680]{0,1:T(8,128)(2,1)} %broadcast_in_dim.10, bf16[280,1680]{0,1:T(8,128)(2,1)S(1)} %bitcast.47, s32[]{:T(128)S(6)} %select_n.98, s32[]{:T(128)} %constant.92.clone.1) | dynamic-update-slice | bytes 1881604 | tf_op jit(solution)/shard_map/dynamic_update_slice | solution.py:13
  195.1 13.1 %dynamic_update_slice.25 = bf16[2240,1680]{0,1:T(8,128)(2,1)} dynamic-update-slice(bf16[2240,1680]{0,1:T(8,128)(2,1)} %dynamic_update_slice.24, bf16[280,1680]{0,1:T(8,128)(2,1)S(1)} %copy.14, s32[]{:T(128)S(6)} %select_n.100, s32[]{:T(128)} %constant.92.clone.1) | dynamic-update-slice | bytes 1881604 | tf_op jit(solution)/shard_map/dynamic_update_slice | solution.py:18
  209.9 13.6 %dynamic_update_slice.26 = bf16[2240,1680]{0,1:T(8,128)(2,1)} dynamic-update-slice(bf16[2240,1680]{0,1:T(8,128)(2,1)} %dynamic_update_slice.25, bf16[280,1680]{0,1:T(8,128)(2,1)S(1)} %copy.15, s32[]{:T(128)S(6)} %select_n.102, s32[]{:T(128)} %constant.92.clone.1) | dynamic-update-slice | bytes 1881604 | tf_op jit(solution)/shard_map/dynamic_update_slice | solution.py:18
  225.2 13.8 %dynamic_update_slice.27 = bf16[2240,1680]{0,1:T(8,128)(2,1)} dynamic-update-slice(bf16[2240,1680]{0,1:T(8,128)(2,1)} %dynamic_update_slice.26, bf16[280,1680]{0,1:T(8,128)(2,1)S(1)} %copy.16, s32[]{:T(128)S(6)} %select_n.104, s32[]{:T(128)} %constant.92.clone.1) | dynamic-update-slice | bytes 1881604 | tf_op jit(solution)/shard_map/dynamic_update_slice | solution.py:18
  240.6 13.8 %dynamic_update_slice.28 = bf16[2240,1680]{0,1:T(8,128)(2,1)} dynamic-update-slice(bf16[2240,1680]{0,1:T(8,128)(2,1)} %dynamic_update_slice.27, bf16[280,1680]{0,1:T(8,128)(2,1)S(1)} %copy.17, s32[]{:T(128)S(6)} %select_n.106, s32[]{:T(128)} %constant.92.clone.1) | dynamic-update-slice | bytes 1881604 | tf_op jit(solution)/shard_map/dynamic_update_slice | solution.py:18
  256.1 13.8 %dynamic_update_slice.29 = bf16[2240,1680]{0,1:T(8,128)(2,1)} dynamic-update-slice(bf16[2240,1680]{0,1:T(8,128)(2,1)} %dynamic_update_slice.28, bf16[280,1680]{0,1:T(8,128)(2,1)S(1)} %copy.18, s32[]{:T(128)S(6)} %select_n.108, s32[]{:T(128)} %constant.92.clone.1) | dynamic-update-slice | bytes 1881604 | tf_op jit(solution)/shard_map/dynamic_update_slice | solution.py:18
  269.9 2.6 copy.19
  272.5 13.8 %dynamic_update_slice.30 = bf16[2240,1680]{0,1:T(8,128)(2,1)} dynamic-update-slice(bf16[2240,1680]{0,1:T(8,128)(2,1)} %dynamic_update_slice.29, bf16[280,1680]{0,1:T(8,128)(2,1)S(1)} %copy.19, s32[]{:T(128)S(6)} %select_n.110, s32[]{:T(128)} %constant.92.clone.1) | dynamic-update-slice | bytes 1881604 | tf_op jit(solution)/shard_map/dynamic_update_slice | solution.py:18
  286.4 2.6 copy.20
  288.9 13.8 %dynamic_update_slice.31 = bf16[2240,1680]{0,1:T(8,128)(2,1)} dynamic-update-slice(bf16[2240,1680]{0,1:T(8,128)(2,1)} %dynamic_update_slice.30, bf16[280,1680]{0,1:T(8,128)(2,1)S(1)} %copy.20, s32[]{:T(128)S(6)} %select_n.112, s32[]{:T(128)} %constant.92.clone.1) | dynamic-update-slice | bytes 1881604 | tf_op jit(solution)/shard_map/dynamic_update_slice | solution.py:18
  302.8 20.8 %convolution_convert_fusion = bf16[1680,1920]{1,0:T(8,128)(2,1)S(1)} fusion(bf16[2240,1680]{0,1:T(8,128)(2,1)} %dynamic_update_slice.31, bf16[1920,2240]{1,0:T(8,128)(2,1)} %bitcast.55), kind=kOutput, calls=%fused_computation.2 | convolution fusion | flops 14453913600 | bytes 22579200 | tf_op jit(solution)/shard_map/dot_general | solution.py:41
  323.6 2.7 copy-done.6
  329.9 31.2 %all-gather.2 = f32[8,5,112]{2,1,0:T(8,128)S(1)} all-gather(f32[1,5,112]{2,1,0:T(8,128)S(1)} %bitcast.54), channel_id=3, replica_groups=mesh['groups'=2,'tm'=8,'space'=2] {'tm'}, dimensions={0}, use_global_device_ids=true | all-gather | bytes 20160 | tf_op jit(solution)/shard_map/all_gather | solution.py:24
  361.1 18.3 %all-gather.8.cloned.1.call-done = f32[40,112,112]{2,1,0:T(8,128)} async-done(((f32[5,112,112]{2,1,0:T(8,128)}), f32[40,112,112]{2,1,0:T(8,128)}) %all-gather.8.cloned.1.call-update) | async-done | bytes 2007056 | tf_op jit(solution)/shard_map/all_gather | solution.py:24
  379.4 7.6 %while.16 = (s32[]{:T(128)}, f32[5,112,112]{2,1,0:T(8,128)S(1)}, f32[5,112]{1,0:T(8,128)S(1)}, s32[]{:T(128)}, f32[8,5,112,112]{3,2,1,0:T(8,128)}, /*index=5*/f32[8,5,112]{2,1,0:T(8,128)S(1)}, s32[]{:T(128)}, s32[]{:T(128)}) while((s32[]{:T(128)}, f32[5,112,112]{2,1,0:T(8,128)S(1)}, f32[5,112]{1,0:T(8,128)S(1)}, s32[]{:T(128)}, ...), condition=%wide.region_2.3_spmd.clone, body=%wide.region_1.2_spmd.clone.sunk | while | flops 189844 | bytes 759475 | solution.py:33
  387.0 2.6 fusion.5
  392.1 8.1 %reshape.34 = bf16[2,12,80,560]{2,1,0,3:T(8,128)(2,1)} reshape(bf16[1920,5,112]{0,2,1:T(8,128)(2,1)S(1)} %fusion) | data formatting | bytes 4300800 | tf_op jit(solution)/shard_map/reshape | solution.py:87
  400.2 6.0 %copy.23 = bf16[2,12,80,560]{3,2,0,1:T(8,128)(2,1)S(1)} copy(bf16[2,12,80,560]{2,1,0,3:T(8,128)(2,1)} %reshape.34) | data formatting | bytes 4300800 | tf_op jit(solution)/shard_map/reshape | solution.py:87
  406.1 5.7 %all_to_all.18 = bf16[2,12,80,560]{3,2,0,1:T(8,128)(2,1)S(1)} all-to-all(bf16[2,12,80,560]{3,2,0,1:T(8,128)(2,1)S(1)} %copy.23), channel_id=1, replica_groups=mesh['groups'=2,'tm'=8,'space'=2] {'space'}, dimensions={1} | all-to-all | bytes 4300800 | tf_op jit(solution)/shard_map/all_to_all | solution.py:88
  411.8 2.5 copy.25
  414.4 2.9 all_to_all.16
  (54 shorter events, 26.8 us)
Async XLA Ops:
  6.5 296.2 %all-gather.6.cloned.1.call-start = ((), (), s32[]{:S(2)}) async-start(), calls=%async_computation.1 | async-start | bytes 13271040 | tf_op jit(solution)/shard_map/all_gather | solution.py:78
  7.3 372.1 %all-gather.8.cloned.1.call-start = ((), (), s32[]{:S(2)}) async-start(), calls=%async_computation.2 | async-start | bytes 2580480 | tf_op jit(solution)/shard_map/all_gather | solution.py:24
  24.0 28.4 %collective-permute-start = (bf16[280,1680]{1,0:T(8,128)(2,1)S(1)}, bf16[280,1680]{1,0:T(8,128)(2,1)S(1)}, u32[]{:S(2)}, u32[]{:S(2)}) collective-permute-start(bf16[280,1680]{1,0:T(8,128)(2,1)S(1)} %copy.13), channel_id=1, source_target_pairs={{0,2},{2,4},{4,6},{6,8},{8,10},{10,12},{12,14},{14,0},{1,3},{3,5},... | collective-permute-start | bytes 2822408 | tf_op jit(solution)/shard_map/ppermute | solution.py:17
  52.4 26.1 %collective-permute-start.1 = (bf16[280,1680]{1,0:T(8,128)(2,1)S(1)}, bf16[280,1680]{1,0:T(8,128)(2,1)S(1)}, u32[]{:S(2)}, u32[]{:S(2)}) collective-permute-start(bf16[280,1680]{1,0:T(8,128)(2,1)S(1)} %collective-permute-done), channel_id=1, source_target_pairs={{0,2},{2,4},{4,6},{6,8},{8,10},{10,12},{12,14},{14,0},{1,3},{3,5},... | collective-permute-start | bytes 2822408 | tf_op jit(solution)/shard_map/ppermute | solution.py:17
  78.5 25.3 %collective-permute-start.2 = (bf16[280,1680]{1,0:T(8,128)(2,1)S(1)}, bf16[280,1680]{1,0:T(8,128)(2,1)S(1)}, u32[]{:S(2)}, u32[]{:S(2)}) collective-permute-start(bf16[280,1680]{1,0:T(8,128)(2,1)S(1)} %collective-permute-done.1), channel_id=1, source_target_pairs={{0,2},{2,4},{4,6},{6,8},{8,10},{10,12},{12,14},{14,0},{1,3},{3,5},... | collective-permute-start | bytes 2822408 | tf_op jit(solution)/shard_map/ppermute | solution.py:17
  103.8 1.0 copy-start
  104.8 24.4 %collective-permute-start.3 = (bf16[280,1680]{1,0:T(8,128)(2,1)S(1)}, bf16[280,1680]{1,0:T(8,128)(2,1)S(1)}, u32[]{:S(2)}, u32[]{:S(2)}) collective-permute-start(bf16[280,1680]{1,0:T(8,128)(2,1)S(1)} %collective-permute-done.2), channel_id=1, source_target_pairs={{0,2},{2,4},{4,6},{6,8},{8,10},{10,12},{12,14},{14,0},{1,3},{3,5},... | collective-permute-start | bytes 2822408 | tf_op jit(solution)/shard_map/ppermute | solution.py:17
  129.2 1.0 copy-start.2
  130.2 23.6 %collective-permute-start.4 = (bf16[280,1680]{1,0:T(8,128)(2,1)S(1)}, bf16[280,1680]{1,0:T(8,128)(2,1)S(1)}, u32[]{:S(2)}, u32[]{:S(2)}) collective-permute-start(bf16[280,1680]{1,0:T(8,128)(2,1)S(1)} %collective-permute-done.3), channel_id=1, source_target_pairs={{0,2},{2,4},{4,6},{6,8},{8,10},{10,12},{12,14},{14,0},{1,3},{3,5},... | collective-permute-start | bytes 2822408 | tf_op jit(solution)/shard_map/ppermute | solution.py:17
  153.7 1.0 copy-start.4
  154.7 22.8 %collective-permute-start.5 = (bf16[280,1680]{1,0:T(8,128)(2,1)S(1)}, bf16[280,1680]{1,0:T(8,128)(2,1)}, u32[]{:S(2)}, u32[]{:S(2)}) collective-permute-start(bf16[280,1680]{1,0:T(8,128)(2,1)S(1)} %collective-permute-done.4), channel_id=1, source_target_pairs={{0,2},{2,4},{4,6},{6,8},{8,10},{10,12},{12,14},{14,0},{1,3},{3,5},... | collective-permute-start | bytes 2822408 | tf_op jit(solution)/shard_map/ppermute | solution.py:17
  177.5 108.8 %collective-permute-start.6 = (bf16[280,1680]{1,0:T(8,128)(2,1)}, bf16[280,1680]{1,0:T(8,128)(2,1)}, u32[]{:S(2)}, u32[]{:S(2)}) collective-permute-start(bf16[280,1680]{1,0:T(8,128)(2,1)} %collective-permute-done.5), channel_id=1, source_target_pairs={{0,2},{2,4},{4,6},{6,8},{8,10},{10,12},{12,14},{14,0},{1,3},{3,5},... | collective-permute-start | bytes 2822408 | tf_op jit(solution)/shard_map/ppermute | solution.py:17
  208.2 15.3 %copy-start.1 = (bf16[280,1680]{1,0:T(8,128)(2,1)S(1)}, bf16[280,1680]{1,0:T(8,128)(2,1)}, u32[]{:S(2)}) copy-start(bf16[280,1680]{1,0:T(8,128)(2,1)} %copy-done) | copy-start | bytes 2822404
  223.5 15.5 %copy-start.3 = (bf16[280,1680]{1,0:T(8,128)(2,1)S(1)}, bf16[280,1680]{1,0:T(8,128)(2,1)}, u32[]{:S(2)}) copy-start(bf16[280,1680]{1,0:T(8,128)(2,1)} %copy-done.2) | copy-start | bytes 2822404
  239.0 15.5 %copy-start.5 = (bf16[280,1680]{1,0:T(8,128)(2,1)S(1)}, bf16[280,1680]{1,0:T(8,128)(2,1)}, u32[]{:S(2)}) copy-start(bf16[280,1680]{1,0:T(8,128)(2,1)} %copy-done.4) | copy-start | bytes 2822404
  323.6 2.7 copy-start.6
  387.0 2.7 copy-start.7
Sparse Core Ops, SparseCore 0:
  8.9 22.1 all-gather.5
  327.9 51.4 all-gather.7
